TPU v7x, 32 devices: a whole 2x2x4 slice. The times are simulated.
32 devices in a mesh: lat: 16 (over z, y, x), field: 2 (over core).
Axes of the slice: x: 2, y: 2, z: 4, core: 2. Of those that a mesh axis runs over, the one named last changes fastest.
Arguments:
- fields_grid: bfloat16 [2, 64, 2, 48, 192], P('field', None, None, 'lat'), may hold values from -6 to 6
- basis: bfloat16 [128, 48, 96], P('lat'), may hold values from -0.875 to 0.875
- order_table: int32 [16, 8], replicated, may hold values from -1 to 95, as said below
- panel_modes: int32 [2, 64], replicated, may hold values from 0 to 95, as said below
Outputs:
- panel: bfloat16 [2, 128, 192, 128], P('field', 'lat')
Inputs may be any that keep to these rules, and one draw needn't show every extreme that they name: `order_table`: each order 0 to 95 stands in exactly one slot; every other slot holds -1; some group has all 8 slots filled. `panel_modes`: row 1 is never smaller than row 0 in the same column; degree 95 appears.
All inputs are finite; a program needn't handle non-finite values.
Results may differ from a plain program's by a relative error of at most 0.0082.
Values may be sent and summed in bfloat16 or wider, within the bound.
A program may use at most 64 MiB of HBM per device.

v0:
```python
import math
import jax
import jax.numpy as jnp
from jax import lax
from jax.sharding import PartitionSpec as P


def dft_table(orders, lon_count):
    valid_slot = orders >= 0
    safe_orders = jnp.maximum(orders, 0)
    products = lax.broadcasted_iota(jnp.int32, (lon_count, 1), 0) * safe_orders[None, :] % lon_count
    angles = products.astype(jnp.float32) * (2.0 * math.pi / lon_count)
    cosine = jnp.where(valid_slot[None, :], jnp.cos(angles), 0.0).astype(jnp.bfloat16)
    sine_table = jnp.where(valid_slot[None, :], -jnp.sin(angles), 0.0).astype(jnp.bfloat16)
    return jnp.stack([cosine, sine_table], axis=1)


def local(fields_grid, basis, order_table, panel_modes):
    grid_one = fields_grid[0]
    snap_count = grid_one.shape[0]
    pair_count = grid_one.shape[2]
    lon_count = grid_one.shape[3]
    slot_count = order_table.shape[1]
    deg_count = basis.shape[2]
    pair_total = basis.shape[1]
    mode_count = panel_modes.shape[1]
    orders = order_table.reshape(-1)
    slot_all = orders.shape[0]
    dft = dft_table(orders, lon_count)
    fourier = jnp.einsum("thjn,nrk->hkjrt", grid_one, dft, preferred_element_type=jnp.float32) * (
        1.0 / math.sqrt(lon_count)
    )
    fourier = fourier.reshape(2, slot_all, pair_count, 2 * snap_count)
    parity_parts = jnp.stack([fourier[0] + fourier[1], fourier[0] - fourier[1]]).astype(
        jnp.bfloat16
    )
    group_index = lax.axis_index("lat")
    my_orders = lax.dynamic_slice_in_dim(order_table, group_index, 1, 0)[0]
    my_odd = my_orders % 2 == 1
    basis_split = basis.reshape(slot_count, pair_total, deg_count // 2, 2)
    even_rows = basis_split[:, :, :, 0]
    odd_rows = basis_split[:, :, :, 1]
    degree = lax.broadcasted_iota(jnp.int32, (1, deg_count), 1)
    keep_mask = (degree >= my_orders[:, None]) & (my_orders >= 0)[:, None]
    received = lax.all_to_all(parity_parts, "lat", split_axis=1, concat_axis=2, tiled=True)
    first_parity = jnp.where(my_odd[:, None, None], received[1], received[0])
    second = jnp.where(my_odd[:, None, None], received[0], received[1])
    low_degrees = jnp.einsum(
        "sjh,sjc->shc", even_rows, first_parity, preferred_element_type=jnp.float32
    )
    high_degrees = jnp.einsum("sjh,sjc->shc", odd_rows, second, preferred_element_type=jnp.float32)
    joined = jnp.stack([low_degrees, high_degrees], axis=2).reshape(slot_count, deg_count, -1)
    coefficients = jnp.where(keep_mask[:, :, None], joined, 0.0).astype(jnp.bfloat16)
    mode_order = panel_modes[0]
    mode_degree = panel_modes[1]
    onehot = (my_orders[None, :] == mode_order[:, None]).astype(jnp.bfloat16)
    picked = jnp.take(coefficients, mode_degree, axis=1)
    local_values = jnp.einsum("ms,smc->mc", onehot, picked, preferred_element_type=jnp.float32)
    field_index = lax.axis_index("field")
    both_fields = jnp.stack(
        [
            jnp.where(field_index == 0, local_values, 0.0),
            jnp.where(field_index == 1, local_values, 0.0),
        ]
    )
    summed = lax.psum(both_fields, ("lat", "field"))
    other_field = jnp.where(field_index == 0, summed[1], summed[0]).astype(jnp.bfloat16)
    columns = other_field.astype(jnp.float32).reshape(mode_count * 2, snap_count)
    centered = (columns - jnp.mean(columns, axis=1, keepdims=True)).astype(jnp.bfloat16)
    coef_rows = coefficients.reshape(slot_count * deg_count * 2, snap_count)
    panel_values = lax.dot_general(
        coef_rows, centered, (((1,), (1,)), ((), ())), preferred_element_type=jnp.float32
    )
    panel_values = panel_values * (1.0 / (snap_count - 1))
    return panel_values.astype(jnp.bfloat16).reshape(1, slot_count, 2 * deg_count, 2 * mode_count)


def solution(mesh):
    placed = (P("field", None, None, "lat", None), P("lat", None, None), P(), P())
    return jax.shard_map(
        local, mesh=mesh, in_specs=placed, out_specs=P("field", "lat", None, None), check_vma=False
    )
```

profile of v0, /device:TPU:0, one launch (start us, length us, event | category | flops | bytes accessed | tf_op | source)
XLA Modules:
  0.0 63.5 jit_solution(17050038539362757233)
XLA Ops:
  0.0 0.0 copy-start.1
  0.0 0.8 %broadcast_compare_fusion = pred[16,8]{0,1:T(8,128)(4,1)S(1)} fusion(s32[16,8]{0,1:T(8,128)} %param.6), kind=kLoop, calls=%fused_computation.57 | loop fusion | flops 128 | bytes 640 | tf_op jit(solution)/shard_map/ge | solution.py:9
  0.8 0.0 copy-done.1
  0.8 0.1 copy.39
  0.9 0.1 ge.51
  1.0 0.1 copy.40
  1.0 0.1 max.11
  1.1 0.4 select_convert_fusion.1
  1.6 1.1 %fusion.1 = f32[2,128,3,2,64]{1,4,2,0,3:T(8,128)S(1)} fusion(bf16[64,2,3,192]{3,1,2,0:T(2,128)(2,1)} %bitcast.69, bf16[192,1,128]{2,0,1:T(8,128)(2,1)S(1)} %get-tuple-element.16, bf16[192,1,128]{2,0,1:T(8,128)(2,1)S(1)} %get-tuple-element.15), kind=kOutput, calls=%fused_computation.4 | convolution fusion | flops 38043648 | bytes 638976 | tf_op jit(solution)/shard_map/thjn,nrk->hkjrt/dot_general | solution.py:30
  2.8 0.8 %copy.44 = bf16[2,128,3,128]{3,0,2,1:T(2,128)(2,1)} copy(bf16[2,128,3,128]{1,3,2,0:T(8,128)(2,1)S(1)} %pad_maximum_fusion.1) | data formatting | bytes 393216 | tf_op jit(solution)/shard_map/stack | solution.py:34
  3.7 0.0 copy-start
  3.7 8.5 %all-to-all-start = ((bf16[2,128,3,128]{3,0,2,1:T(2,128)(2,1)}), bf16[2,128,3,128]{3,0,2,1:T(2,128)(2,1)S(1)}, u32[]{:S(2)}, u32[]{:S(2)}) async-start(bf16[2,128,3,128]{3,0,2,1:T(2,128)(2,1)} %copy.44), calls=%async_computation | async-start | bytes 393216 | tf_op jit(solution)/shard_map/all_to_all | solution.py:45
  12.1 0.0 copy-start.2
  12.2 0.7 %copy-done.2 = s32[2,64]{1,0:T(2,128)S(1)} copy-done((s32[2,64]{1,0:T(2,128)S(1)}, s32[2,64]{1,0:T(2,128)}, u32[]{:S(2)}) %copy-start.2) | copy-done | bytes 536
  12.8 0.2 dynamic-slice_reduce_fusion
  13.0 0.1 compare_bitcast_fusion
  13.2 0.0 copy-done
  13.2 0.2 copy.48
  13.4 7.4 %all-to-all-done = bf16[2,128,3,128]{3,0,2,1:T(2,128)(2,1)S(1)} async-done(((bf16[2,128,3,128]{3,0,2,1:T(2,128)(2,1)}), bf16[2,128,3,128]{3,0,2,1:T(2,128)(2,1)S(1)}, u32[]{:S(2)}, u32[]{:S(2)}) %all-to-all-start) | async-done | bytes 196640 | tf_op jit(solution)/shard_map/all_to_all | solution.py:45
  20.9 0.1 bitcast_select_fusion.2
  21.0 0.2 convolution_bitcast_fusion.1
  21.2 0.2 convolution_bitcast_fusion
  21.4 0.1 copy.53
  21.5 0.2 fusion.2
  21.7 0.6 gather_fusion
  22.3 0.3 fusion.5
  22.6 39.0 %psum.7 = bf16[2,64,128]{2,1,0:T(8,128)(2,1)S(1)} all-reduce(f32[2,64,128]{2,1,0:T(8,128)S(1)} %pad_maximum_fusion.2), channel_id=1, replica_groups=mesh['lat'=16,'field'=2] {'lat','field'}, use_global_device_ids=true, to_apply=%region_0.1 | all-reduce | flops 16384 | bytes 98304 | tf_op jit(solution)/shard_map/psum | solution.py:66
  61.6 0.1 reshape.345
  61.7 0.1 reduce_sum.9
  61.8 0.1 div.10
  62.0 0.1 sub.26
  62.1 0.1 sub.27
  62.2 0.1 convert_element_type.92
  62.3 0.2 convert_element_type.86
  62.5 1.0 %fusion = bf16[1536,128]{1,0:T(8,128)(2,1)} fusion(bf16[1536,64]{1,0:T(8,128)(2,1)S(1)} %convert_element_type.86, bf16[128,64]{1,0:T(8,128)(2,1)S(1)} %convert_element_type.92), kind=kOutput, calls=%fused_computation.2 | convolution fusion | flops 25559040 | bytes 606208 | tf_op jit(solution)/shard_map/dot_general | solution.py:71
  (23 shorter events, 0.3 us)
Async XLA Ops:
  0.0 0.8 %copy-start.1 = (s32[16,8]{0,1:T(8,128)S(1)}, s32[16,8]{0,1:T(8,128)}, u32[]{:S(2)}) copy-start(s32[16,8]{0,1:T(8,128)} %param.6) | copy-start | bytes 1540
  3.7 9.5 %copy-start = (bf16[8,48,96]{2,1,0:T(8,128)(2,1)S(1)}, bf16[8,48,96]{2,1,0:T(8,128)(2,1)}, u32[]{:S(2)}) copy-start(bf16[8,48,96]{2,1,0:T(8,128)(2,1)} %param.5) | copy-start | bytes 221188
  3.7 17.1 %all-to-all-start = ((bf16[2,128,3,128]{3,0,2,1:T(2,128)(2,1)}), bf16[2,128,3,128]{3,0,2,1:T(2,128)(2,1)S(1)}, u32[]{:S(2)}, u32[]{:S(2)}) async-start(bf16[2,128,3,128]{3,0,2,1:T(2,128)(2,1)} %copy.44), calls=%async_computation | async-start | bytes 393216 | tf_op jit(solution)/shard_map/all_to_all | solution.py:45
  12.1 0.7 %copy-start.2 = (s32[2,64]{1,0:T(2,128)S(1)}, s32[2,64]{1,0:T(2,128)}, u32[]{:S(2)}) copy-start(s32[2,64]{1,0:T(2,128)} %param.7) | copy-start | bytes 1540
where the time goes:
time: 63.9 us; the launch traced here: 63.5 us
  blocking collectives  39 us (61%)
  starting transfers between devices  8.47 us (13%)
  waiting for transfers between devices  7.41 us (12%)
  local copies, waits for them, and re-layouts  3.74 us (6%)
  matrix products  2.79 us (4%)
  other arithmetic  1.84 us (3%)
    psum x1, blocking collectives, local(): summed = lax.psum(both_fields, ('lat', 'field'))  39 us
    all_to_all x1, starting transfers between devices, local(): lax.all_to_all(parity_parts, 'lat', split_axis=1, concat_axis=2, tiled=True)  8.47 us
    all_to_all x1, waiting for transfers between devices, local(): lax.all_to_all(parity_parts, 'lat', split_axis=1, concat_axis=2, tiled=True)  7.41 us
  transfers between devices with their start and end apart: 1, of which 1 were waited for; matrix products, arithmetic and copies ran while one was open for 1% of the time, Pallas kernels for 0%

commit v1 on v0

--- a/solution.py
+++ b/solution.py
@@ -63,7 +63,7 @@
             jnp.where(field_index == 1, local_values, 0.0),
         ]
     )
-    summed = lax.psum(both_fields, ("lat", "field"))
+    summed = jnp.sum(jax.lax.all_gather(both_fields, ("lat", "field")), axis=0)
     other_field = jnp.where(field_index == 0, summed[1], summed[0]).astype(jnp.bfloat16)
     columns = other_field.astype(jnp.float32).reshape(mode_count * 2, snap_count)
     centered = (columns - jnp.mean(columns, axis=1, keepdims=True)).astype(jnp.bfloat16)

time: 63.9 us -> 95 us (1.49)
  waiting for transfers between devices: 7.41 us -> 61.9 us
  blocking collectives: 39 us -> 0 us
  between operations: 0.28 us -> 13.7 us
  other arithmetic: 1.84 us -> 4.86 us
    all_gather x0 -> x1, waiting for transfers between devices: none -> 53.9 us  [local(): summed = jnp.sum(jax.lax.all_gather(both_fields, ('lat', 'field')), axis=0)]
    psum x1 -> x0, blocking collectives: 39 us -> none  [local(): summed = lax.psum(both_fields, ('lat', 'field'))]
    reduce_sum x0 -> x1, other arithmetic: none -> 1.7 us  [local(): summed = jnp.sum(jax.lax.all_gather(both_fields, ('lat', 'field')), axis=0)]
  transfers between devices with their start and end apart: 1 -> 2, of which waited for: 1 -> 2; matrix products, arithmetic and copies ran while one was open for 1% -> 1% of each run, Pallas kernels for 0% -> 0%
where the time goes in v1:
time: 95 us; the launch traced here: 94.7 us
  waiting for transfers between devices  61.9 us (65%)
  between operations  13.7 us (14%)
  starting transfers between devices  8.38 us (9%)
  other arithmetic  4.86 us (5%)
  local copies, waits for them, and re-layouts  3.08 us (3%)
  matrix products  2.79 us (3%)
    all_gather x1, waiting for transfers between devices, local(): summed = jnp.sum(jax.lax.all_gather(both_fields, ('lat', 'field')), axis=0)  53.9 us
    all_to_all x1, starting transfers between devices, local(): lax.all_to_all(parity_parts, 'lat', split_axis=1, concat_axis=2, tiled=True)  8.34 us
    all_to_all x1, waiting for transfers between devices, local(): lax.all_to_all(parity_parts, 'lat', split_axis=1, concat_axis=2, tiled=True)  8 us
  transfers between devices with their start and end apart: 2, of which 2 were waited for; matrix products, arithmetic and copies ran while one was open for 1% of the time, Pallas kernels for 0%

profile of v1, /device:TPU:0, one launch (start us, length us, event | category | flops | bytes accessed | tf_op | source)
XLA Modules:
  0.0 94.7 jit_solution(6620204686136337275)
XLA Ops:
  6.5 0.0 copy-start.1
  6.5 0.0 copy-start.2
  6.5 0.0 copy-start
  6.5 0.8 broadcast_compare_fusion
  7.3 0.7 broadcast_maximum_fusion
  8.0 0.1 copy.39
  8.1 0.1 ge.51
  8.2 0.1 copy.40
  8.2 0.1 max.11
  8.3 0.4 select_convert_fusion.1
  8.8 1.1 %fusion.1 = f32[2,128,3,2,64]{1,4,2,0,3:T(8,128)S(1)} fusion(bf16[64,2,3,192]{3,1,2,0:T(2,128)(2,1)} %bitcast.71, bf16[192,1,128]{2,0,1:T(8,128)(2,1)S(1)} %get-tuple-element.16, bf16[192,1,128]{2,0,1:T(8,128)(2,1)S(1)} %get-tuple-element.15), kind=kOutput, calls=%fused_computation.4 | convolution fusion | flops 38043648 | bytes 638976 | tf_op jit(solution)/shard_map/thjn,nrk->hkjrt/dot_general | solution.py:30
  10.0 0.8 copy.44
  10.9 8.3 %all-to-all-start = ((bf16[2,128,3,128]{3,0,2,1:T(2,128)(2,1)}), bf16[2,128,3,128]{3,0,2,1:T(2,128)(2,1)S(1)}, u32[]{:S(2)}, u32[]{:S(2)}) async-start(bf16[2,128,3,128]{3,0,2,1:T(2,128)(2,1)} %copy.44), calls=%async_computation | async-start | bytes 393216 | tf_op jit(solution)/shard_map/all_to_all | solution.py:45
  19.2 0.0 all-gather.3.cloned.1.call-start
  19.3 0.0 copy-done.2
  19.3 0.0 copy-done.1
  19.3 0.2 dynamic-slice_reduce_fusion
  19.5 0.1 compare_bitcast_fusion
  19.6 0.0 copy-done
  19.7 0.2 copy.48
  19.9 8.0 %all-to-all-done = bf16[2,128,3,128]{3,0,2,1:T(2,128)(2,1)S(1)} async-done(((bf16[2,128,3,128]{3,0,2,1:T(2,128)(2,1)}), bf16[2,128,3,128]{3,0,2,1:T(2,128)(2,1)S(1)}, u32[]{:S(2)}, u32[]{:S(2)}) %all-to-all-start) | async-done | bytes 196640 | tf_op jit(solution)/shard_map/all_to_all | solution.py:45
  28.0 0.1 bitcast_select_fusion.2
  28.1 0.2 convolution_bitcast_fusion.1
  28.3 0.2 convolution_bitcast_fusion
  28.5 0.1 copy.53
  28.5 0.2 fusion.2
  28.7 0.6 gather_fusion
  29.4 0.3 fusion.5
  29.6 0.6 pad_maximum_fusion.2
  30.3 0.0 all-gather.3.cloned.1.call-update
  30.3 0.2 convert_element_type.86
  30.5 53.9 %all-gather.3.cloned.1.call-done = f32[64,64,128]{2,1,0:T(8,128)} async-done(((f32[2,64,128]{2,1,0:T(8,128)}), f32[64,64,128]{2,1,0:T(8,128)}) %all-gather.3.cloned.1.call-update) | async-done | bytes 2097168 | tf_op jit(solution)/shard_map/all_gather | solution.py:66
  84.4 1.7 %reduce_sum.18 = bf16[2,64,128]{2,1,0:T(8,128)(2,1)S(1)} reduce(f32[32,2,64,128]{3,2,1,0:T(8,128)} %bitcast.66, f32[]{:T(128)} %constant.60.clone.1), dimensions={0}, to_apply=%region_0.1 | reduce | flops 507904 | bytes 2129924 | tf_op jit(solution)/shard_map/reduce_sum | solution.py:66
  86.1 0.1 reshape.345
  86.2 0.1 reduce_sum.19
  86.3 0.1 div.10
  86.5 0.1 sub.26
  86.6 0.1 sub.27
  86.7 0.1 convert_element_type.92
  86.8 1.0 %fusion = bf16[1536,128]{1,0:T(8,128)(2,1)} fusion(bf16[1536,64]{1,0:T(8,128)(2,1)S(1)} %convert_element_type.86, bf16[128,64]{1,0:T(8,128)(2,1)S(1)} %convert_element_type.92), kind=kOutput, calls=%fused_computation.2 | convolution fusion | flops 25559040 | bytes 606208 | tf_op jit(solution)/shard_map/dot_general | solution.py:71
  (21 shorter events, 0.3 us)
Async XLA Ops:
  6.5 12.8 %copy-start.1 = (s32[16,8]{0,1:T(8,128)S(1)}, s32[16,8]{0,1:T(8,128)}, u32[]{:S(2)}) copy-start(s32[16,8]{0,1:T(8,128)} %param.6) | copy-start | bytes 1540
  6.5 12.7 %copy-start.2 = (s32[2,64]{1,0:T(2,128)S(1)}, s32[2,64]{1,0:T(2,128)}, u32[]{:S(2)}) copy-start(s32[2,64]{1,0:T(2,128)} %param.7) | copy-start | bytes 1540
  6.5 13.1 %copy-start = (bf16[8,48,96]{2,1,0:T(8,128)(2,1)S(1)}, bf16[8,48,96]{2,1,0:T(8,128)(2,1)}, u32[]{:S(2)}) copy-start(bf16[8,48,96]{2,1,0:T(8,128)(2,1)} %param.5) | copy-start | bytes 221188
  10.9 17.0 %all-to-all-start = ((bf16[2,128,3,128]{3,0,2,1:T(2,128)(2,1)}), bf16[2,128,3,128]{3,0,2,1:T(2,128)(2,1)S(1)}, u32[]{:S(2)}, u32[]{:S(2)}) async-start(bf16[2,128,3,128]{3,0,2,1:T(2,128)(2,1)} %copy.44), calls=%async_computation | async-start | bytes 393216 | tf_op jit(solution)/shard_map/all_to_all | solution.py:45
  19.2 65.2 %all-gather.3.cloned.1.call-start = ((), (), s32[]{:S(2)}) async-start(), calls=%async_computation.1 | async-start | bytes 2162688 | tf_op jit(solution)/shard_map/all_gather | solution.py:66
Sparse Core Ops, SparseCore 0:
  30.4 53.9 all-gather.2
